TPU v7x, 512 devices: a whole 4x8x8 slice. The times are simulated.
512 devices in a mesh: seq: 64 (over z, x, core), head: 8 (over y).
Axes of the slice: x: 4, y: 8, z: 8, core: 2. Of those that a mesh axis runs over, the one named last changes fastest.
Arguments:
- query_proj: bfloat16 [65536, 512], P(('seq', 'head')), may hold values from -4 to 4
- key_proj: bfloat16 [65536, 512], P(('seq', 'head')), may hold values from -8 to 8
- value_proj: bfloat16 [65536, 4096], P(('seq', 'head')), may hold values from -6.5 to 6.5
- conv_query: float32 [3, 512], replicated, may hold values from -1 to 1
- conv_key: float32 [3, 512], replicated, may hold values from -1 to 1
- conv_value: float32 [3, 4096], replicated, may hold values from -1 to 1
Outputs:
- mixed_out: bfloat16 [65536, 4096], P(('seq', 'head'))
All inputs are finite; a program needn't handle non-finite values.
Results may differ from a plain program's by a relative error of at most 0.0027.
Values may be sent and summed in bfloat16 or wider, within the bound.
A program may use at most 128 MiB of HBM per device.

v0:
```python
import jax
import jax.numpy as jnp
import numpy as np
from jax import lax
from jax.sharding import PartitionSpec as P

KD = 16
VD = 128
SPAN = 128
KERNEL = 3


def carried_in(part, axis, combine, identity):
    place = lax.axis_index(axis)
    gathered = jax.tree.map(lambda a: lax.all_gather(a, axis), part)
    state = jax.tree.map(lambda a, e: jnp.zeros_like(a) + jnp.asarray(e, a.dtype), part, identity)

    def one(step, state):
        return combine(
            state, jax.tree.map(lambda a: lax.dynamic_index_in_dim(a, step, 0, False), gathered)
        )

    return lax.fori_loop(0, place, one, state)


def passed_along(shard, axis, by):
    size = lax.axis_size(axis)
    pairs = [(i, i + by) for i in range(size) if 0 <= i + by < size]
    return lax.ppermute(shard, axis, pairs)


def features(values):
    scaled = values * KD ** (-0.25)
    first_index, second_index = np.triu_indices(KD, 1)
    cross = scaled[..., first_index] * scaled[..., second_index]
    return jnp.concatenate(
        [jnp.ones_like(scaled[..., :1]), scaled, scaled * scaled * 0.5**0.5, cross], axis=-1
    )


def convolve_rows(row_block, before, tap_rows):
    joined = jnp.concatenate([before, row_block], axis=0).astype(jnp.float32)
    length = row_block.shape[0]
    width = tap_rows.shape[0]
    summed = jnp.zeros((length, row_block.shape[1]), jnp.float32)
    for offset in range(width):
        start = width - 1 - offset
        summed = summed + tap_rows[offset] * joined[start : start + length]
    return summed


def combine_sums(earlier, later):
    return (earlier[0] + later[0], earlier[1] + later[1])


def carried_sums(total_state, total_norm):
    identity = (jnp.zeros_like(total_state), jnp.zeros_like(total_norm))
    return carried_in((total_state, total_norm), "seq", combine_sums, identity)


def state_terms(query_float, state_part, norm_part):
    numer_term = jnp.einsum(
        "nchf,nhfv->nchv",
        query_float,
        state_part,
        precision=lax.Precision.HIGHEST,
        preferred_element_type=jnp.float32,
    )
    denom_term = jnp.einsum(
        "nchf,nhf->nch",
        query_float,
        norm_part,
        precision=lax.Precision.HIGHEST,
        preferred_element_type=jnp.float32,
    )
    return (numer_term, denom_term)


def on_device(query_proj, key_proj, value_proj, conv_query, conv_key, conv_value):
    margin = KERNEL - 1
    query_rows, key_rows, value_rows = (
        lax.all_to_all(query_proj, "head", split_axis=1, concat_axis=0, tiled=True),
        lax.all_to_all(key_proj, "head", split_axis=1, concat_axis=0, tiled=True),
        lax.all_to_all(value_proj, "head", split_axis=1, concat_axis=0, tiled=True),
    )
    group_count = lax.axis_size("head")
    group_index = lax.axis_index("head")
    head_count = query_proj.shape[1] // KD // group_count
    taps_query = lax.dynamic_slice_in_dim(
        conv_query, group_index * head_count * KD, head_count * KD, 1
    )
    taps_key = lax.dynamic_slice_in_dim(conv_key, group_index * head_count * KD, head_count * KD, 1)
    taps_value = lax.dynamic_slice_in_dim(
        conv_value, group_index * head_count * VD, head_count * VD, 1
    )
    before = passed_along(
        (query_rows[-margin:], key_rows[-margin:], value_rows[-margin:]), "seq", 1
    )
    query_conv = convolve_rows(query_rows, before[0], taps_query)
    key_conv = convolve_rows(key_rows, before[1], taps_key)
    value_conv = convolve_rows(value_rows, before[2], taps_value).astype(jnp.bfloat16)
    length = query_conv.shape[0]
    block_count = length // SPAN
    query_feat = features(query_conv.reshape(block_count, SPAN, head_count, KD)).astype(
        jnp.bfloat16
    )
    key_feat = features(key_conv.reshape(block_count, SPAN, head_count, KD)).astype(jnp.bfloat16)
    value_block = value_conv.reshape(block_count, SPAN, head_count, VD)
    causal = jnp.arange(SPAN)[:, None] >= jnp.arange(SPAN)[None, :]
    scores = jnp.einsum("nchf,nmhf->nhcm", query_feat, key_feat, preferred_element_type=jnp.float32)
    scores = jnp.where(causal, scores, jnp.float32(0.0))
    inner_den = jnp.sum(scores, axis=-1).transpose(0, 2, 1)
    inner_num = jnp.einsum(
        "nhcm,nmhv->nchv",
        scores.astype(jnp.bfloat16),
        value_block,
        preferred_element_type=jnp.float32,
    )
    block_state = jnp.einsum(
        "nmhf,nmhv->nhfv", key_feat, value_block, preferred_element_type=jnp.float32
    )
    block_norm = jnp.sum(key_feat.astype(jnp.float32), axis=1)
    prefix_state = jnp.concatenate(
        [jnp.zeros_like(block_state[:1]), jnp.cumsum(block_state, axis=0)[:-1]], axis=0
    )
    prefix_norm = jnp.concatenate(
        [jnp.zeros_like(block_norm[:1]), jnp.cumsum(block_norm, axis=0)[:-1]], axis=0
    )
    total_state = prefix_state[-1] + block_state[-1]
    total_norm = prefix_norm[-1] + block_norm[-1]
    query_float = query_feat.astype(jnp.float32)
    numer_term, denom_term = state_terms(query_float, prefix_state, prefix_norm)
    numerator = inner_num + numer_term
    denominator = inner_den + denom_term
    device_state, device_norm = carried_sums(total_state, total_norm)
    numerator = numerator + jnp.einsum(
        "nchf,hfv->nchv",
        query_float,
        device_state,
        precision=lax.Precision.HIGHEST,
        preferred_element_type=jnp.float32,
    )
    denominator = denominator + jnp.einsum(
        "nchf,hf->nch",
        query_float,
        device_norm,
        precision=lax.Precision.HIGHEST,
        preferred_element_type=jnp.float32,
    )
    result_rows = (
        (numerator / denominator[..., None]).astype(jnp.bfloat16).reshape(length, head_count * VD)
    )
    result_rows = lax.all_to_all(result_rows, "head", split_axis=0, concat_axis=1, tiled=True)
    return result_rows


def solution(mesh):
    in_specs = (
        P(("seq", "head"), None),
        P(("seq", "head"), None),
        P(("seq", "head"), None),
        P(),
        P(),
        P(),
    )
    out_specs = P(("seq", "head"), None)
    return jax.shard_map(
        on_device, mesh=mesh, in_specs=in_specs, out_specs=out_specs, check_vma=False
    )
```

profile of v0, /device:TPU:455, one launch (start us, length us, event | category | flops | bytes accessed | tf_op | source)
XLA Modules:
  0.0 331.2 jit_solution(399916114119146279)
XLA Ops:
  8.2 6.8 %all-to-all-start.2 = ((bf16[128,8,64]{0,2,1:T(8,128)(2,1)}), bf16[128,8,64]{0,2,1:T(8,128)(2,1)S(1)}, u32[]{:S(2)}, u32[]{:S(2)}) async-start(bf16[128,8,64]{0,2,1:T(8,128)(2,1)} %bitcast.15), calls=%async_computation.2 | async-start | bytes 262144 | tf_op jit(solution)/shard_map/all_to_all | solution.py:83
  15.0 2.3 copy.62
  17.3 5.5 %all-to-all-done.2 = bf16[128,8,64]{0,2,1:T(8,128)(2,1)S(1)} async-done(((bf16[128,8,64]{0,2,1:T(8,128)(2,1)}), bf16[128,8,64]{0,2,1:T(8,128)(2,1)S(1)}, u32[]{:S(2)}, u32[]{:S(2)}) %all-to-all-start.2) | async-done | bytes 131104 | tf_op jit(solution)/shard_map/all_to_all | solution.py:83
  22.8 3.6 %all-to-all-start = ((bf16[128,8,512]{0,2,1:T(8,128)(2,1)}), bf16[128,8,512]{0,2,1:T(8,128)(2,1)S(1)}, u32[]{:S(2)}, u32[]{:S(2)}) async-start(bf16[128,8,512]{0,2,1:T(8,128)(2,1)} %bitcast.3), calls=%async_computation | async-start | bytes 2097152 | tf_op jit(solution)/shard_map/all_to_all | solution.py:84
  29.5 3.5 %collective-permute-done.2 = bf16[2,64]{0,1:T(8,128)(2,1)S(1)} collective-permute-done((bf16[2,64]{0,1:T(8,128)(2,1)S(1)}, bf16[2,64]{0,1:T(8,128)(2,1)S(1)}, u32[]{:S(2)}, u32[]{:S(2)}) %collective-permute-start.2) | collective-permute-done | bytes 288 | tf_op jit(solution)/shard_map/ppermute | solution.py:29
  34.3 2.1 gather_fusion.3
  36.4 4.7 %fusion.16 = bf16[8,128,4,120]{1,3,2,0:T(8,128)(2,1)} fusion(f32[120,8,128,4]{2,1,3,0:T(8,128)} %gather_fusion.3, f32[120,8,128,4]{2,1,3,0:T(8,128)S(1)} %gather_fusion.2), kind=kLoop, calls=%fused_computation.35 | loop fusion | flops 983040 | bytes 4915200 | tf_op jit(solution)/shard_map/convert.3
  41.1 14.3 %all-to-all-done = bf16[128,8,512]{0,2,1:T(8,128)(2,1)S(1)} async-done(((bf16[128,8,512]{0,2,1:T(8,128)(2,1)}), bf16[128,8,512]{0,2,1:T(8,128)(2,1)S(1)}, u32[]{:S(2)}, u32[]{:S(2)}) %all-to-all-start) | async-done | bytes 1048608 | tf_op jit(solution)/shard_map/all_to_all | solution.py:84
  57.4 1.7 collective-permute-done
  62.0 2.3 fusion.34
  66.1 3.4 %all-to-all-start.1 = ((bf16[128,8,64]{0,2,1:T(8,128)(2,1)}), bf16[128,8,64]{0,2,1:T(8,128)(2,1)S(1)}, u32[]{:S(2)}, u32[]{:S(2)}) async-start(bf16[128,8,64]{0,2,1:T(8,128)(2,1)} %bitcast.9), calls=%async_computation.1 | async-start | bytes 262144 | tf_op jit(solution)/shard_map/all_to_all | solution.py:82
  69.5 7.9 %all-to-all-done.1 = bf16[128,8,64]{0,2,1:T(8,128)(2,1)S(1)} async-done(((bf16[128,8,64]{0,2,1:T(8,128)(2,1)}), bf16[128,8,64]{0,2,1:T(8,128)(2,1)S(1)}, u32[]{:S(2)}, u32[]{:S(2)}) %all-to-all-start.1) | async-done | bytes 131104 | tf_op jit(solution)/shard_map/all_to_all | solution.py:82
  78.8 4.7 %collective-permute-done.1 = bf16[2,64]{0,1:T(8,128)(2,1)S(1)} collective-permute-done((bf16[2,64]{0,1:T(8,128)(2,1)S(1)}, bf16[2,64]{0,1:T(8,128)(2,1)S(1)}, u32[]{:S(2)}, u32[]{:S(2)}) %collective-permute-start.1) | collective-permute-done | bytes 288 | tf_op jit(solution)/shard_map/ppermute | solution.py:29
  83.9 2.1 gather_fusion
  86.0 2.1 gather_fusion.1
  88.2 2.6 convert_reduce_fusion
  90.8 51.5 %all_gather.9 = f32[64,4,153]{2,1,0:T(4,128)} all-gather(f32[1,4,153]{2,1,0:T(4,128)S(1)} %slice_add_fusion.1), channel_id=1, replica_groups=mesh['seq'=64,'head'=8] {'seq'}, dimensions={0}, use_global_device_ids=true | all-gather | bytes 159120 | tf_op jit(solution)/shard_map/all_gather | solution.py:15
  142.4 3.7 %fusion.15 = bf16[8,128,4,120]{1,3,2,0:T(8,128)(2,1)S(1)} fusion(f32[120,8,128,4]{2,1,3,0:T(8,128)} %gather_fusion.1, f32[120,8,128,4]{2,1,3,0:T(8,128)S(1)} %copy-done.2), kind=kLoop, calls=%fused_computation.34 | loop fusion | flops 983040 | bytes 4915200 | tf_op jit(solution)/shard_map/convert.7
  149.4 1.9 fusion.12
  151.3 4.7 %fusion.1 = f32[8,4,128,128]{3,2,1,0:T(8,128)} fusion(bf16[8,128,4,153]{1,3,2,0:T(8,128)(2,1)S(1)} %pad_maximum_fusion, f32[8,4,153,128]{3,2,1,0:T(8,128)S(1)} %fusion.34), kind=kOutput, calls=%fused_computation.9 | convolution fusion | flops 842268672 | bytes 5701632 | tf_op jit(solution)/shard_map/nchf,nhfv->nchv/dot_general | solution.py:62
  156.0 16.8 %all-gather.2.cloned.1.call-done = f32[64,4,153,128]{3,1,2,0:T(4,128)} async-done(((f32[1,4,153,128]{3,1,2,0:T(4,128)}), f32[64,4,153,128]{3,1,2,0:T(4,128)}) %all-gather.2.cloned.1.call-update) | async-done | bytes 20054032 | tf_op jit(solution)/shard_map/all_gather | solution.py:15
  172.8 111.9 %while.12 = (s32[]{:T(128)}, f32[4,153,128]{2,1,0:T(8,128)S(1)}, f32[4,153]{1,0:T(4,128)S(1)}, s32[]{:T(128)}, f32[64,4,153,128]{3,1,2,0:T(4,128)}, /*index=5*/f...) while((s32[]{:T(128)}, f32[4,153,128]{2,1,0:T(8,128)S(1)}, f32[4,153]{1,0:T(4,128)S(1)}, s32[]{:T(128)}, ...), condition=%wide.region_4.5_spmd, body=%wide.region_3.4_spmd.sunk | while | flops 78953 | bytes 1574199 | solution.py:23
  285.3 3.5 %fusion.7 = bf16[8,128,4,128]{1,3,2,0:T(8,128)(2,1)S(1)} fusion(f32[8,4,128,128]{3,2,1,0:T(8,128)} %fusion.12, f32[8,4,128,128]{3,2,1,0:T(8,128)} %fusion.1, bf16[8,128,4,153]{1,3,2,0:T(8,128)(2,1)S(1)} %copy-done.1, f32[8,128,4]{1,2,0:T(4,128)S(1)} %bitcast_add_fusion.2, f32[4,153,128]{2,1,0:T(8,128)S(1)} %get-tuple-element.39), kind=kOutput, calls=%fused_computation.19 | convolution fusion | flops 964689920 | bytes 6825984 | tf_op jit(solution)/shard_map/nchf,hfv->nchv/dot_general | solution.py:136
  288.8 34.3 %all_to_all.76 = bf16[8,128,512]{1,2,0:T(8,128)(2,1)S(1)} all-to-all(bf16[8,128,512]{1,2,0:T(8,128)(2,1)S(1)} %bitcast.103), channel_id=1, replica_groups=mesh['seq'=64,'head'=8] {'head'}, dimensions={0} | all-to-all | bytes 2097152 | tf_op jit(solution)/shard_map/all_to_all | solution.py:153
  (259 shorter events, 130.8 us)
Async XLA Ops:
  8.2 14.6 %all-to-all-start.2 = ((bf16[128,8,64]{0,2,1:T(8,128)(2,1)}), bf16[128,8,64]{0,2,1:T(8,128)(2,1)S(1)}, u32[]{:S(2)}, u32[]{:S(2)}) async-start(bf16[128,8,64]{0,2,1:T(8,128)(2,1)} %bitcast.15), calls=%async_computation.2 | async-start | bytes 262144 | tf_op jit(solution)/shard_map/all_to_all | solution.py:83
  15.0 11.4 %copy-start.9 = (s32[120]{0:T(128)S(1)}, s32[120]{0:T(128)}, u32[]{:S(2)}) copy-start(s32[120]{0:T(128)} %constant.72) | copy-start | bytes 1444
  15.0 14.5 %copy-start.8 = (s32[120]{0:T(128)S(1)}, s32[120]{0:T(128)}, u32[]{:S(2)}) copy-start(s32[120]{0:T(128)} %constant.73) | copy-start | bytes 1444
  22.8 32.6 %all-to-all-start = ((bf16[128,8,512]{0,2,1:T(8,128)(2,1)}), bf16[128,8,512]{0,2,1:T(8,128)(2,1)S(1)}, u32[]{:S(2)}, u32[]{:S(2)}) async-start(bf16[128,8,512]{0,2,1:T(8,128)(2,1)} %bitcast.3), calls=%async_computation | async-start | bytes 2097152 | tf_op jit(solution)/shard_map/all_to_all | solution.py:84
  26.4 146.4 %all-gather.2.cloned.1.call-start = ((), (), s32[]{:S(2)}) async-start(), calls=%async_computation.4 | async-start | bytes 20367360 | tf_op jit(solution)/shard_map/all_gather | solution.py:15
  28.2 4.8 %collective-permute-start.2 = (bf16[2,64]{0,1:T(8,128)(2,1)S(1)}, bf16[2,64]{0,1:T(8,128)(2,1)S(1)}, u32[]{:S(2)}, u32[]{:S(2)}) collective-permute-start(bf16[2,64]{0,1:T(8,128)(2,1)S(1)} %slice.126), channel_id=1, source_target_pairs={{0,8},{8,16},{16,24},{24,32},{32,40},{40,48},{48,56},{56,64},{64,7... | collective-permute-start | bytes 776 | tf_op jit(solution)/shard_map/ppermute | solution.py:29
  55.9 3.1 collective-permute-start
  60.0 1.3 copy-start.5
  60.3 1.0 copy-start.3
  62.0 3.3 %copy-start.7 = (bf16[128,512]{1,0:T(8,128)(2,1)S(1)}, bf16[128,512]{1,0:T(8,128)(2,1)}, u32[]{:S(2)}) copy-start(bf16[128,512]{1,0:T(8,128)(2,1)} %param.16) | copy-start | bytes 393220
  66.1 11.3 %all-to-all-start.1 = ((bf16[128,8,64]{0,2,1:T(8,128)(2,1)}), bf16[128,8,64]{0,2,1:T(8,128)(2,1)S(1)}, u32[]{:S(2)}, u32[]{:S(2)}) async-start(bf16[128,8,64]{0,2,1:T(8,128)(2,1)} %bitcast.9), calls=%async_computation.1 | async-start | bytes 262144 | tf_op jit(solution)/shard_map/all_to_all | solution.py:82
  77.5 6.0 %collective-permute-start.1 = (bf16[2,64]{0,1:T(8,128)(2,1)S(1)}, bf16[2,64]{0,1:T(8,128)(2,1)S(1)}, u32[]{:S(2)}, u32[]{:S(2)}) collective-permute-start(bf16[2,64]{0,1:T(8,128)(2,1)S(1)} %slice.122), channel_id=1, source_target_pairs={{0,8},{8,16},{16,24},{24,32},{32,40},{40,48},{48,56},{56,64},{64,7... | collective-permute-start | bytes 776 | tf_op jit(solution)/shard_map/ppermute | solution.py:29
  88.1 54.3 %copy-start.2 = (f32[120,8,128,4]{2,1,3,0:T(8,128)S(1)}, f32[120,8,128,4]{2,1,3,0:T(8,128)}, u32[]{:S(2)}) copy-start(f32[120,8,128,4]{2,1,3,0:T(8,128)} %gather_fusion) | copy-start | bytes 5898244
  146.1 1.7 copy-start.6
  146.7 4.6 %copy-start = (bf16[8,128,4,153]{1,3,2,0:T(8,128)(2,1)}, bf16[8,128,4,153]{1,3,2,0:T(8,128)(2,1)S(1)}, u32[]{:S(2)}) copy-start(bf16[8,128,4,153]{1,3,2,0:T(8,128)(2,1)S(1)} %pad_maximum_fusion) | copy-start | bytes 3760132
  147.9 1.5 copy-start.4
  172.8 111.9 %copy-start.1 = (bf16[8,128,4,153]{1,3,2,0:T(8,128)(2,1)S(1)}, bf16[8,128,4,153]{1,3,2,0:T(8,128)(2,1)}, u32[]{:S(2)}) copy-start(bf16[8,128,4,153]{1,3,2,0:T(8,128)(2,1)} %copy-done) | copy-start | bytes 3760132
Sparse Core Ops, SparseCore 0:
  65.5 107.2 all-gather.1
where the time goes:
time: 336 us; the launch traced here: 331 us
  blocking collectives  85.8 us (26%)
  local copies, waits for them, and re-layouts  80.8 us (24%)
  other arithmetic  64.5 us (19%)
  waiting for transfers between devices  54.4 us (16%)
  starting transfers between devices  17.6 us (5%)
  between operations  13.8 us (4%)
  matrix products  13.6 us (4%)
    dynamic_slice x63, local copies, waits for them, and re-layouts, one(): lax.dynamic_index_in_dim(a, step, 0, False)  62.4 us
    all_gather x1, blocking collectives, carried_in(): gathered = jax.tree.map(lambda a: lax.all_gather(a, axis), part)  51.5 us
    add x126, other arithmetic, combine_sums(): return (earlier[0] + later[0], earlier[1] + later[1])  48.7 us
    all_to_all x1, blocking collectives, on_device(): lax.all_to_all(result_rows, 'head', split_axis=0, concat_axis=1, tiled=True)  34.3 us
    all_gather x1, waiting for transfers between devices, carried_in(): gathered = jax.tree.map(lambda a: lax.all_gather(a, axis), part)  16.8 us
    all_to_all x1, waiting for transfers between devices, on_device(): lax.all_to_all(value_proj, 'head', split_axis=1, concat_axis=0, tiled=True)  14.3 us
    ppermute x3, waiting for transfers between devices, passed_along(): return lax.ppermute(shard, axis, pairs)  9.88 us
    another operation x4, other arithmetic  8.56 us
  transfers between devices with their start and end apart: 7, of which 7 were waited for; matrix products, arithmetic and copies ran while one was open for 10% of the time, Pallas kernels for 0%

commit v1 on v0

v1 whole, which is shorter than its diff:
```python
import functools

import jax
import jax.numpy as jnp
from jax import lax
from jax.experimental import pallas as pl
from jax.experimental.pallas import tpu as pltpu
from jax.sharding import PartitionSpec as P

KD = 16
VD = 128
SPAN = 128
KERNEL = 3
HALO = 16
FEAT = 160
PLANE = 8
MESH = pl.DeviceIdType.MESH


def features(rows):
    parts = [rows, rows * rows * (0.5**0.5)]
    for step in range(1, KD // 2):
        parts.append(rows * jnp.concatenate([rows[step:], rows[:step]], axis=0))
    parts.append(rows[: KD // 2] * rows[KD // 2 :])
    index = lax.broadcasted_iota(jnp.int32, (8, rows.shape[1]), 0)
    parts.append(jnp.where(index == 0, 1.0, 0.0).astype(jnp.float32))
    return jnp.concatenate(parts, axis=0)


def convolve(block, before, taps):
    row = lax.broadcasted_iota(jnp.int32, block.shape, 0)
    last = before[HALO - 1 : HALO]
    second = before[HALO - 2 : HALO - 1]
    one = jnp.where(row == 0, last, pltpu.roll(block, 1, 0))
    two = jnp.where(row == 0, second, jnp.where(row == 1, last, pltpu.roll(block, 2, 0)))
    return taps[0:1] * block + taps[1:2] * one + taps[2:3] * two


def split(value):
    high = value.astype(jnp.bfloat16)
    return high, (value - high.astype(jnp.float32)).astype(jnp.bfloat16)


def dot(a, b):
    return jnp.dot(a, b, preferred_element_type=jnp.float32)


def kernel(
    shards,
    groups,
    heads,
    qk_hbm,
    v_hbm,
    taps_qk,
    taps_v,
    out_hbm,
    qk_in,
    v_in,
    key_feat,
    query_feat,
    value,
    before_state,
    numer,
    denom,
    total,
    slices,
    plane,
    others,
    carried,
    prefixes,
    carry,
    result,
    qk_send,
    qk_recv,
    v_send,
    v_recv,
    halo_send,
    halo_recv,
    one_send,
    one_recv,
    two_send,
    two_recv,
    three_send,
    three_recv,
    out_send,
    out_recv,
    own_sem,
):
    s = lax.axis_index("seq")
    y = lax.axis_index("head")
    z = s // PLANE
    r = s % PLANE
    layers = shards // PLANE
    width = heads * VD
    part = slices.shape[1]

    def y_peer(step):
        return (y + step) % groups

    def r_peer(step):
        return (r + step) % PLANE

    following = (s + 1) % shards
    preceding = (s + shards - 1) % shards

    barrier = pltpu.get_barrier_semaphore()
    greet = [(s, y_peer(d)) for d in range(1, groups)]
    greet += [(z * PLANE + r_peer(d), y) for d in range(1, PLANE)]
    greet += [(((z + d) % layers) * PLANE + r, y) for d in range(1, layers)]
    greet += [(following, y), (preceding, y)]
    for place in greet:
        pl.semaphore_signal(barrier, inc=1, device_id=place, device_id_type=MESH)
    pl.semaphore_wait(barrier, len(greet))

    def columns(group):
        return pl.ds(pl.multiple_of(group * width, width), width)

    def remote(src, dst, send, recv, place):
        return pltpu.make_async_remote_copy(
            src_ref=src,
            dst_ref=dst,
            send_sem=send,
            recv_sem=recv,
            device_id=place,
            device_id_type=MESH,
        )

    def send_qk(peer, owner, semaphore):
        return remote(
            qk_hbm.at[peer], qk_in.at[owner + 1], qk_send.at[peer], qk_recv.at[semaphore], (s, peer)
        )

    def send_v(peer, owner, semaphore):
        return remote(
            v_hbm.at[:, columns(peer)],
            v_in.at[owner + 1],
            v_send.at[peer],
            v_recv.at[semaphore],
            (s, peer),
        )

    for d in range(1, groups):
        send_qk(y_peer(d), y, y).start()
    for d in range(1, groups):
        send_v(y_peer(d), y, y).start()
    own_qk = pltpu.make_async_copy(qk_hbm.at[y], qk_in.at[y + 1], own_sem.at[0])
    own_v = pltpu.make_async_copy(v_hbm.at[:, columns(y)], v_in.at[y + 1], own_sem.at[1])
    own_qk.start()
    own_v.start()
    own_qk.wait()
    own_v.wait()
    for d in range(1, groups):
        send_qk(y_peer(d), y_peer(d), y_peer(d)).wait_recv()
    for d in range(1, groups):
        send_v(y_peer(d), y_peer(d), y_peer(d)).wait_recv()

    tail = pl.ds(SPAN - HALO, HALO)
    halo_qk = remote(
        qk_in.at[groups, tail],
        qk_in.at[0, tail],
        halo_send.at[0],
        halo_recv.at[0],
        (following, y),
    )
    halo_v = remote(
        v_in.at[groups, tail], v_in.at[0, tail], halo_send.at[1], halo_recv.at[1], (following, y)
    )
    halo_qk.start()
    halo_v.start()
    halo_qk.wait()
    halo_v.wait()

    total[...] = jnp.zeros_like(total)
    lane = lax.broadcasted_iota(jnp.int32, (FEAT, VD), 1)

    def summarize(n, _):
        keep = jnp.logical_or(n > 0, s > 0)
        qk_before = jnp.where(keep, qk_in[n, SPAN - HALO :].astype(jnp.float32), 0.0)
        v_before = jnp.where(keep, v_in[n, SPAN - HALO :].astype(jnp.float32), 0.0)
        qk = convolve(qk_in[n + 1].astype(jnp.float32), qk_before, taps_qk[y])
        rows = (qk * KD**-0.25).T
        mixed = convolve(v_in[n + 1].astype(jnp.float32), v_before, taps_v[:, columns(y)])
        mixed = mixed.astype(jnp.bfloat16)
        norms = total[heads * FEAT : (heads + 1) * FEAT]
        for h in range(heads):
            query = features(rows[h * KD : (h + 1) * KD])
            key = features(rows[(heads + h) * KD : (heads + h + 1) * KD]).astype(jnp.bfloat16)
            own = mixed[:, h * VD : (h + 1) * VD]
            query_feat[h, n] = query.T.astype(jnp.bfloat16)
            key_feat[h, n] = key
            value[h, n] = own
            both = jnp.concatenate([own, jnp.ones_like(own)], axis=1)
            added = dot(key, both)
            state = total[h * FEAT : (h + 1) * FEAT]
            before_state[h, n, :, :VD] = state
            before_state[h, n, :, VD:] = jnp.broadcast_to(
                norms[:, h * 32 : h * 32 + 1], (FEAT, VD)
            )
            total[h * FEAT : (h + 1) * FEAT] = state + added[:, :VD]
            norms = norms + jnp.where(lane // 32 == h, added[:, VD:], 0.0)
        total[heads * FEAT : (heads + 1) * FEAT] = norms
        return 0

    lax.fori_loop(0, groups, summarize, 0)

    def piece(ref, index):
        return ref.at[pl.ds(pl.multiple_of(index * part, 8), part)]

    def send_one(peer, owner):
        return remote(
            piece(total, peer),
            slices.at[owner],
            one_send.at[peer],
            one_recv.at[owner],
            (z * PLANE + peer, y),
        )

    for d in range(1, PLANE):
        send_one(r_peer(d), r).start()
    slices[r] = total[pl.ds(pl.multiple_of(r * part, 8), part)]

    causal = lax.broadcasted_iota(jnp.int32, (SPAN, SPAN), 0) >= lax.broadcasted_iota(
        jnp.int32, (SPAN, SPAN), 1
    )

    def attend(h):
        def one(n, _):
            query = query_feat[h, n]
            scores = jnp.where(causal, dot(query, key_feat[h, n]), 0.0)
            high, low = split(before_state[h, n])
            earlier = dot(query, high) + dot(query, low)
            numer[h, n] = dot(scores.astype(jnp.bfloat16), value[h, n]) + earlier[:, :VD]
            denom[h, n] = jnp.sum(scores, axis=1, keepdims=True) + earlier[:, VD:]
            return 0

        lax.fori_loop(0, groups, one, 0)

    attend(0)
    attend(1)

    for d in range(1, PLANE):
        send_one(r_peer(d), r_peer(d)).wait_recv()
    running = slices[0]
    for other in range(1, PLANE):
        running = running + slices[other]
    plane[...] = running

    def send_two(to, owner):
        return remote(
            plane, others.at[owner], two_send.at[to], two_recv.at[owner], (to * PLANE + r, y)
        )

    for to in range(1, layers):

        @pl.when(z < to)
        def _():
            send_two(to, z).start()

    attend(2)

    carried[...] = jnp.zeros_like(carried)
    for owner in range(layers - 1):

        @pl.when(owner < z)
        def _():
            send_two(z, owner).wait_recv()
            carried[...] += others[owner]

    running = carried[...]
    prefixes[0] = running
    for other in range(1, PLANE):
        running = running + slices[other - 1]
        prefixes[other] = running

    def send_three(peer, owner):
        return remote(
            prefixes.at[peer],
            piece(carry, owner),
            three_send.at[peer],
            three_recv.at[owner],
            (z * PLANE + peer, y),
        )

    for d in range(1, PLANE):
        send_three(r_peer(d), r).start()
    carry[pl.ds(pl.multiple_of(r * part, 8), part)] = prefixes[r]

    for h in range(3, heads):
        attend(h)

    for d in range(1, PLANE):
        send_three(r_peer(d), r_peer(d)).wait_recv()

    def send_out(peer, owner):
        return remote(
            result.at[peer],
            out_hbm.at[:, columns(owner)],
            out_send.at[peer],
            out_recv.at[owner],
            (s, peer),
        )

    carry_parts = []
    for h in range(heads):
        column = carry[heads * FEAT : (heads + 1) * FEAT][:, h * 32 : h * 32 + 1]
        both = jnp.concatenate(
            [carry[h * FEAT : (h + 1) * FEAT], jnp.broadcast_to(column, (FEAT, VD))], axis=1
        )
        high, low = split(both)
        carry_parts.append((high, low))

    def finish(n):
        for h in range(heads):
            query = query_feat[h, n]
            earlier = dot(query, carry_parts[h][0]) + dot(query, carry_parts[h][1])
            mixed = (numer[h, n] + earlier[:, :VD]) / (denom[h, n] + earlier[:, VD:])
            result[n, :, h * VD : (h + 1) * VD] = mixed.astype(jnp.bfloat16)

    def finish_and_send(step, _):
        peer = y_peer(step)
        finish(peer)
        send_out(peer, y).start()
        return 0

    lax.fori_loop(1, groups, finish_and_send, 0)
    finish(y)
    own_out = pltpu.make_async_copy(result.at[y], out_hbm.at[:, columns(y)], own_sem.at[2])
    own_out.start()

    for d in range(1, groups):
        send_qk(y_peer(d), y, y).wait_send()
        send_v(y_peer(d), y, y).wait_send()
    for d in range(1, PLANE):
        send_one(r_peer(d), r).wait_send()
        send_three(r_peer(d), r).wait_send()
    for to in range(1, layers):

        @pl.when(z < to)
        def _():
            send_two(to, z).wait_send()

    own_out.wait()
    for d in range(1, groups):
        send_out(y_peer(d), y).wait_send()
        send_out(y_peer(d), y_peer(d)).wait_recv()


def on_device(shards, groups, query_proj, key_proj, value_proj, conv_query, conv_key, conv_value):
    tokens = query_proj.shape[0]
    heads = query_proj.shape[1] // KD // groups

    def grouped(query, key):
        rows = query.shape[0]
        both = jnp.concatenate(
            [query.reshape(rows, groups, heads * KD), key.reshape(rows, groups, heads * KD)],
            axis=2,
        )
        return both.transpose(1, 0, 2)

    qk = grouped(query_proj, key_proj)
    taps_qk = grouped(conv_query, conv_key)
    rows = (heads + 1) * FEAT
    part = -(-rows // (8 * PLANE)) * 8
    layers = shards // PLANE
    scratch = pltpu.VMEM
    dma = pltpu.SemaphoreType.DMA
    f32, bf16 = jnp.float32, jnp.bfloat16
    return pl.pallas_call(
        functools.partial(kernel, shards, groups, heads),
        out_shape=jax.ShapeDtypeStruct(value_proj.shape, bf16),
        in_specs=[
            pl.BlockSpec(memory_space=pl.ANY),
            pl.BlockSpec(memory_space=pl.ANY),
            pl.BlockSpec(memory_space=pltpu.VMEM),
            pl.BlockSpec(memory_space=pltpu.VMEM),
        ],
        out_specs=pl.BlockSpec(memory_space=pl.ANY),
        scratch_shapes=[
            scratch((groups + 1, tokens, 2 * heads * KD), bf16),
            scratch((groups + 1, tokens, heads * VD), bf16),
            scratch((heads, groups, FEAT, SPAN), bf16),
            scratch((heads, groups, SPAN, FEAT), bf16),
            scratch((heads, groups, SPAN, VD), bf16),
            scratch((heads, groups, FEAT, 2 * VD), f32),
            scratch((heads, groups, SPAN, VD), f32),
            scratch((heads, groups, SPAN, VD), f32),
            scratch((part * PLANE, VD), f32),
            scratch((PLANE, part, VD), f32),
            scratch((part, VD), f32),
            scratch((layers, part, VD), f32),
            scratch((part, VD), f32),
            scratch((PLANE, part, VD), f32),
            scratch((part * PLANE, VD), f32),
            scratch((groups, tokens, heads * VD), bf16),
            dma((groups,)),
            dma((groups,)),
            dma((groups,)),
            dma((groups,)),
            dma((2,)),
            dma((2,)),
            dma((PLANE,)),
            dma((PLANE,)),
            dma((layers,)),
            dma((layers,)),
            dma((PLANE,)),
            dma((PLANE,)),
            dma((groups,)),
            dma((groups,)),
            dma((3,)),
        ],
        compiler_params=pltpu.CompilerParams(collective_id=0, has_side_effects=True),
    )(qk, value_proj, taps_qk, conv_value)


def solution(mesh):
    shards, groups = mesh.shape["seq"], mesh.shape["head"]
    rows = P(("seq", "head"), None)
    return jax.shard_map(
        functools.partial(on_device, shards, groups),
        mesh=mesh,
        in_specs=(rows, rows, rows, P(), P(), P()),
        out_specs=rows,
        check_vma=False,
    )
```

time: 336 us -> 105 us (0.31)
  the two profiles are of different devices: /device:TPU:455 before, /device:TPU:1 now
where the time goes in v1:
time: 105 us
  Pallas kernels  98.1 us (93%)
  local copies, waits for them, and re-layouts  5.2 us (5%)
  other arithmetic  1.53 us (1%)
    pallas_call x1, Pallas kernels, on_device(): pl.pallas_call(functools.partial(kernel, shards, groups, heads), out_shap...  98.1 us
    unnamed x7, local copies, waits for them, and re-layouts  3.24 us

profile of v1, /device:TPU:1, one launch (start us, length us, event | category | flops | bytes accessed | tf_op | source)
XLA Modules:
  0.0 104.9 jit_solution(11321171519141121702)
XLA Ops:
  0.0 0.0 copy-start
  0.0 0.8 reshape.14
  0.8 0.8 reshape.15
  1.6 0.7 maximum_bitcast_fusion.1.taps_qk
  2.3 0.0 copy-done
  2.3 0.1 copy.7
  2.4 0.0 copy-start.1
  2.4 0.2 copy.9
  2.6 0.7 copy-done.1
  3.3 0.1 copy.8
  3.4 0.2 copy.10
  3.6 0.9 maximum_bitcast_fusion.qk_hbm
  4.5 98.1 %shard_map.64 = bf16[128,4096]{1,0:T(8,128)(2,1)} custom-call(bf16[8,128,128]{2,1,0:T(8,128)(2,1)} %maximum_bitcast_fusion.qk_hbm, bf16[128,4096]{1,0:T(8,128)(2,1)} %v_hbm.1, f32[8,3,128]{2,1,0:T(4,128)} %maximum_bitcast_fusion.1.taps_qk, f32[3,4096]{1,0:T(4,128)} %taps_v.1), custom_call_target="tpu_custom_call" | custom-call | tf_op jit(solution)/shard_map/pallas_call | solution.py:368
  102.6 2.3 %copy.14 = bf16[128,4096]{1,0:T(8,128)(2,1)} copy(bf16[128,4096]{1,0:T(8,128)(2,1)} %shard_map.64) | data formatting | bytes 2097152
  (2 shorter events, 0.0 us)
Async XLA Ops:
  0.0 2.3 %copy-start = (bf16[128,512]{1,0:T(8,128)(2,1)S(1)}, bf16[128,512]{1,0:T(8,128)(2,1)}, u32[]{:S(2)}) copy-start(bf16[128,512]{1,0:T(8,128)(2,1)} %param.6) | copy-start | bytes 393220
  2.4 0.9 copy-start.1

commit v2 on v1

v2 whole, which is shorter than its diff:
```python
import functools

import jax
import jax.numpy as jnp
from jax import lax
from jax.experimental import pallas as pl
from jax.experimental.pallas import tpu as pltpu
from jax.sharding import PartitionSpec as P

KD = 16
VD = 128
SPAN = 128
KERNEL = 3
HALO = 16
FEAT = 160
PLANE = 8
MESH = pl.DeviceIdType.MESH


def features(rows):
    parts = [rows, rows * rows * (0.5**0.5)]
    for step in range(1, KD // 2):
        parts.append(rows * jnp.concatenate([rows[step:], rows[:step]], axis=0))
    parts.append(rows[: KD // 2] * rows[KD // 2 :])
    index = lax.broadcasted_iota(jnp.int32, (8, rows.shape[1]), 0)
    parts.append(jnp.where(index == 0, 1.0, 0.0).astype(jnp.float32))
    return jnp.concatenate(parts, axis=0)


def convolve(block, before, taps):
    row = lax.broadcasted_iota(jnp.int32, block.shape, 0)
    last = before[HALO - 1 : HALO]
    second = before[HALO - 2 : HALO - 1]
    one = jnp.where(row == 0, last, pltpu.roll(block, 1, 0))
    two = jnp.where(row == 0, second, jnp.where(row == 1, last, pltpu.roll(block, 2, 0)))
    return taps[0:1] * block + taps[1:2] * one + taps[2:3] * two


def split(value):
    high = value.astype(jnp.bfloat16)
    return high, (value - high.astype(jnp.float32)).astype(jnp.bfloat16)


def dot(a, b):
    return jnp.dot(a, b, preferred_element_type=jnp.float32)


def kernel(
    shards,
    groups,
    heads,
    query_ref,
    key_ref,
    v_hbm,
    taps_query,
    taps_key,
    taps_v,
    out_hbm,
    qk_out,
    qk_in,
    v_in,
    v_halo,
    taps_qk,
    key_feat,
    query_feat,
    value,
    before_state,
    numer,
    denom,
    total,
    slices,
    plane,
    others,
    carried,
    prefixes,
    carry,
    result,
    qk_send,
    qk_recv,
    v_send,
    v_recv,
    halo_send,
    halo_recv,
    one_send,
    one_recv,
    two_send,
    two_recv,
    three_send,
    three_recv,
    out_send,
    out_recv,
    own_qk_sem,
    own_v_sem,
    own_out_sem,
):
    s = lax.axis_index("seq")
    y = lax.axis_index("head")
    z = s // PLANE
    r = s % PLANE
    layers = shards // PLANE
    last = groups - 1
    near = heads * KD

    def y_peer(step):
        return (y + step) % groups

    def r_peer(step):
        return (r + step) % PLANE

    following = (s + 1) % shards
    preceding = (s + shards - 1) % shards
    order = sorted(range(1, groups), key=lambda step: min(step, groups - step))

    barrier = pltpu.get_barrier_semaphore()
    greet = [(s, y_peer(d)) for d in order]
    greet += [(z * PLANE + r_peer(d), y) for d in range(1, PLANE)]
    greet += [(((z + d) % layers) * PLANE + r, y) for d in range(1, layers)]
    for place in greet + [(preceding, last)]:
        pl.semaphore_signal(barrier, inc=1, device_id=place, device_id_type=MESH)

    for g in range(groups):
        own = slice(g * near, (g + 1) * near)
        qk_out[g] = jnp.concatenate([query_ref[:, own], key_ref[:, own]], axis=1)
        taps_qk[g, :KERNEL] = jnp.concatenate([taps_query[:, own], taps_key[:, own]], axis=1)

    @pl.when(y == last)
    def _():
        pl.semaphore_wait(barrier, len(greet) + groups)

    @pl.when(y != last)
    def _():
        pl.semaphore_wait(barrier, len(greet))

    def columns(group, h):
        return pl.ds(pl.multiple_of((group * heads + h) * VD, VD), VD)

    def wide(group):
        return pl.ds(pl.multiple_of(group * heads * VD, heads * VD), heads * VD)

    def remote(src, dst, send, recv, place):
        return pltpu.make_async_remote_copy(
            src_ref=src,
            dst_ref=dst,
            send_sem=send,
            recv_sem=recv,
            device_id=place,
            device_id_type=MESH,
        )

    tail = pl.ds(SPAN - HALO, HALO)

    def send_halo_qk(group):
        return remote(
            qk_out.at[group, tail],
            qk_in.at[0, tail],
            halo_send.at[0, group],
            halo_recv.at[0],
            (following, group),
        )

    def send_halo_v(group):
        return remote(
            v_hbm.at[tail, wide(group)],
            v_halo,
            halo_send.at[1, group],
            halo_recv.at[1],
            (following, group),
        )

    def send_qk(peer, owner):
        return remote(
            qk_out.at[peer], qk_in.at[owner + 1], qk_send.at[peer], qk_recv.at[owner], (s, peer)
        )

    def send_v(h, peer, owner):
        return remote(
            v_hbm.at[:, columns(peer, h)],
            v_in.at[h, owner],
            v_send.at[h, peer],
            v_recv.at[h, owner],
            (s, peer),
        )

    def own_v(h):
        return pltpu.make_async_copy(v_hbm.at[:, columns(y, h)], v_in.at[h, y], own_v_sem.at[h])

    own_qk = pltpu.make_async_copy(qk_out.at[y], qk_in.at[y + 1], own_qk_sem.at[0])
    for d in order:
        send_qk(y_peer(d), y).start()

    @pl.when(y == last)
    def _():
        for group in range(groups):
            send_halo_qk(group).start()
            send_halo_v(group).start()

    own_qk.start()
    for h in range(heads):
        for d in order:
            send_v(h, y_peer(d), y).start()
        own_v(h).start()

    total[...] = jnp.zeros_like(total)
    own_qk.wait()
    for d in order:
        send_qk(y_peer(d), y_peer(d)).wait_recv()
    send_halo_qk(y).wait_recv()

    def expand(n, _):
        keep = jnp.logical_or(n > 0, s > 0)
        before = jnp.where(keep, qk_in[n, SPAN - HALO :].astype(jnp.float32), 0.0)
        qk = convolve(qk_in[n + 1].astype(jnp.float32), before, taps_qk[y, :KERNEL])
        rows = (qk * KD**-0.25).T
        for h in range(heads):
            query = features(rows[h * KD : (h + 1) * KD])
            key = features(rows[near + h * KD : near + (h + 1) * KD])
            query_feat[h, n] = query.T.astype(jnp.bfloat16)
            key_feat[h, n] = key.astype(jnp.bfloat16)
        return 0

    lax.fori_loop(0, groups, expand, 0)
    send_halo_v(y).wait_recv()

    def summarize(h):
        own_v(h).wait()
        for d in order:
            send_v(h, y_peer(d), y_peer(d)).wait_recv()
        taps = taps_v[:, columns(y, h)]
        state = jnp.zeros((FEAT, 2 * VD), jnp.float32)
        for n in range(groups):
            if n == 0:
                before = v_halo[:, pl.ds(pl.multiple_of(h * VD, VD), VD)].astype(jnp.float32)
                before = jnp.where(s > 0, before, 0.0)
            else:
                before = v_in[h, n - 1, SPAN - HALO :].astype(jnp.float32)
            own = convolve(v_in[h, n].astype(jnp.float32), before, taps).astype(jnp.bfloat16)
            value[h, n] = own
            before_state[h, n] = state
            both = jnp.concatenate([own, jnp.ones_like(own)], axis=1)
            state = state + dot(key_feat[h, n], both)
        norm = state[:, VD:].T[:8]
        total[h, :FEAT] = state[:, :VD]
        total[h, FEAT : FEAT + 8] = norm[:, :VD]
        total[h, FEAT + 8 : FEAT + 16, : FEAT - VD] = norm[:, VD:]

    part = total.shape[1] // PLANE

    def piece(index):
        return pl.ds(pl.multiple_of(index * part, 8), part)

    def send_one(h, peer, owner):
        return remote(
            total.at[h, piece(peer)],
            slices.at[h, owner],
            one_send.at[h, peer],
            one_recv.at[h, owner],
            (z * PLANE + peer, y),
        )

    def start_one(h):
        for d in range(1, PLANE):
            send_one(h, r_peer(d), r).start()
        slices[h, r] = total[h, piece(r)]

    def send_two(h, to, owner):
        return remote(
            plane.at[h],
            others.at[h, owner],
            two_send.at[h, to],
            two_recv.at[h, owner],
            (to * PLANE + r, y),
        )

    def start_two(h):
        for d in range(1, PLANE):
            send_one(h, r_peer(d), r_peer(d)).wait_recv()
        running = slices[h, 0]
        for other in range(1, PLANE):
            running = running + slices[h, other]
        plane[h] = running
        for to in range(1, layers):

            @pl.when(z < to)
            def _():
                send_two(h, to, z).start()

    def send_three(h, peer, owner):
        return remote(
            prefixes.at[h, peer],
            carry.at[h, piece(owner)],
            three_send.at[h, peer],
            three_recv.at[h, owner],
            (z * PLANE + peer, y),
        )

    def start_three(h):
        carried[...] = jnp.zeros_like(carried)
        for owner in range(layers - 1):

            @pl.when(owner < z)
            def _():
                send_two(h, z, owner).wait_recv()
                carried[...] += others[h, owner]

        running = carried[...]
        prefixes[h, 0] = running
        for other in range(1, PLANE):
            running = running + slices[h, other - 1]
            prefixes[h, other] = running
        for d in range(1, PLANE):
            send_three(h, r_peer(d), r).start()
        carry[h, piece(r)] = prefixes[h, r]

    causal = lax.broadcasted_iota(jnp.int32, (SPAN, SPAN), 0) >= lax.broadcasted_iota(
        jnp.int32, (SPAN, SPAN), 1
    )

    def attend(h):
        for n in range(groups):
            query = query_feat[h, n]
            scores = jnp.where(causal, dot(query, key_feat[h, n]), 0.0)
            high, low = split(before_state[h, n])
            earlier = dot(query, high) + dot(query, low)
            numer[h, n] = dot(scores.astype(jnp.bfloat16), value[h, n]) + earlier[:, :VD]
            denom[h, n] = jnp.sum(scores, axis=1, keepdims=True) + earlier[:, VD:]

    def send_out(h, peer, owner):
        return remote(
            result.at[h, peer],
            out_hbm.at[:, columns(owner, h)],
            out_send.at[h, peer],
            out_recv.at[h, owner],
            (s, peer),
        )

    def own_out(h):
        return pltpu.make_async_copy(
            result.at[h, y], out_hbm.at[:, columns(y, h)], own_out_sem.at[h]
        )

    def finish(h):
        for d in range(1, PLANE):
            send_three(h, r_peer(d), r_peer(d)).wait_recv()
        norm = jnp.concatenate(
            [carry[h, FEAT : FEAT + 8], carry[h, FEAT + 8 : FEAT + 16][:, : FEAT - VD]], axis=1
        )
        norm = jnp.broadcast_to(norm[:1], (VD, FEAT)).T
        high, low = split(jnp.concatenate([carry[h, :FEAT], norm], axis=1))
        for d in order + [0]:
            n = y_peer(d)
            query = query_feat[h, n]
            earlier = dot(query, high) + dot(query, low)
            mixed = (numer[h, n] + earlier[:, :VD]) / (denom[h, n] + earlier[:, VD:])
            result[h, n] = mixed.astype(jnp.bfloat16)
            if d:
                send_out(h, n, y).start()
        own_out(h).start()

    summarize(0)
    start_one(0)
    attend(0)
    start_two(0)

    def one_head(h, _):
        summarize(h)
        start_one(h)
        start_three(h - 1)
        attend(h)
        start_two(h)
        finish(h - 1)
        return 0

    lax.fori_loop(1, heads, one_head, 0)
    start_three(heads - 1)
    finish(heads - 1)

    for d in order:
        send_qk(y_peer(d), y).wait_send()

    @pl.when(y == last)
    def _():
        for group in range(groups):
            send_halo_qk(group).wait_send()
            send_halo_v(group).wait_send()

    def drain(h, _):
        for d in order:
            send_v(h, y_peer(d), y).wait_send()
        for d in range(1, PLANE):
            send_one(h, r_peer(d), r).wait_send()
            send_three(h, r_peer(d), r).wait_send()
        for to in range(1, layers):

            @pl.when(z < to)
            def _():
                send_two(h, to, z).wait_send()

        own_out(h).wait()
        for d in order:
            send_out(h, y_peer(d), y).wait_send()
            send_out(h, y_peer(d), y_peer(d)).wait_recv()
        return 0

    lax.fori_loop(0, heads, drain, 0)


def on_device(shards, groups, query_proj, key_proj, value_proj, conv_query, conv_key, conv_value):
    tokens = query_proj.shape[0]
    heads = query_proj.shape[1] // KD // groups
    rows = -(-(FEAT + 16) // (8 * PLANE)) * 8 * PLANE
    part = rows // PLANE
    layers = shards // PLANE
    scratch = pltpu.VMEM
    dma = pltpu.SemaphoreType.DMA
    f32, bf16 = jnp.float32, jnp.bfloat16
    whole = pl.BlockSpec(memory_space=pltpu.VMEM)
    return pl.pallas_call(
        functools.partial(kernel, shards, groups, heads),
        out_shape=jax.ShapeDtypeStruct(value_proj.shape, bf16),
        in_specs=[whole, whole, pl.BlockSpec(memory_space=pl.ANY), whole, whole, whole],
        out_specs=pl.BlockSpec(memory_space=pl.ANY),
        scratch_shapes=[
            scratch((groups, tokens, 2 * heads * KD), bf16),
            scratch((groups + 1, tokens, 2 * heads * KD), bf16),
            scratch((heads, groups, tokens, VD), bf16),
            scratch((HALO, heads * VD), bf16),
            scratch((groups, 8, 2 * heads * KD), f32),
            scratch((heads, groups, FEAT, SPAN), bf16),
            scratch((heads, groups, SPAN, FEAT), bf16),
            scratch((heads, groups, SPAN, VD), bf16),
            scratch((heads, groups, FEAT, 2 * VD), f32),
            scratch((heads, groups, SPAN, VD), f32),
            scratch((heads, groups, SPAN, VD), f32),
            scratch((heads, rows, VD), f32),
            scratch((heads, PLANE, part, VD), f32),
            scratch((heads, part, VD), f32),
            scratch((heads, layers, part, VD), f32),
            scratch((part, VD), f32),
            scratch((heads, PLANE, part, VD), f32),
            scratch((heads, rows, VD), f32),
            scratch((heads, groups, tokens, VD), bf16),
            dma((groups,)),
            dma((groups,)),
            dma((heads, groups)),
            dma((heads, groups)),
            dma((2, groups)),
            dma((2,)),
            dma((heads, PLANE)),
            dma((heads, PLANE)),
            dma((heads, layers)),
            dma((heads, layers)),
            dma((heads, PLANE)),
            dma((heads, PLANE)),
            dma((heads, groups)),
            dma((heads, groups)),
            dma((1,)),
            dma((heads,)),
            dma((heads,)),
        ],
        compiler_params=pltpu.CompilerParams(collective_id=0, has_side_effects=True),
    )(query_proj, key_proj, value_proj, conv_query, conv_key, conv_value)


def solution(mesh):
    shards, groups = mesh.shape["seq"], mesh.shape["head"]
    rows = P(("seq", "head"), None)
    return jax.shard_map(
        functools.partial(on_device, shards, groups),
        mesh=mesh,
        in_specs=(rows, rows, rows, P(), P(), P()),
        out_specs=rows,
        check_vma=False,
    )
```

time: 105 us -> 77.2 us (0.74)
  Pallas kernels: 98.1 us -> 74.7 us
  local copies, waits for them, and re-layouts: 5.2 us -> 2.29 us
  other arithmetic: 1.53 us -> 0 us
    pallas_call x1, Pallas kernels: 98.1 us -> 74.7 us  [on_device(): pl.pallas_call(functools.partial(kernel, shards, groups, heads), out_shap...]
    reshape x6 -> x0, local copies, waits for them, and re-layouts: 1.96 us -> none  [the longest x3 1 us: grouped(): query.reshape(rows, groups, heads * KD)]
    transpose x2 -> x0, other arithmetic: 1.53 us -> none  [grouped(): return both.transpose(1, 0, 2)]
    unnamed x7 -> x1, local copies, waits for them, and re-layouts: 3.24 us -> 2.29 us
where the time goes in v2:
time: 77.2 us; the launch traced here: 77 us
  Pallas kernels  74.7 us (97%)
  local copies, waits for them, and re-layouts  2.29 us (3%)
    pallas_call x1, Pallas kernels, on_device(): pl.pallas_call(functools.partial(kernel, shards, groups, heads), out_shap...  74.7 us
    unnamed x1, local copies, waits for them, and re-layouts  2.29 us

profile of v2, /device:TPU:1, one launch (start us, length us, event | category | flops | bytes accessed | tf_op | source)
XLA Modules:
  0.0 77.0 jit_solution(3697738504010006069)
XLA Ops:
  0.0 74.7 %shard_map.64 = bf16[128,4096]{1,0:T(8,128)(2,1)} custom-call(bf16[128,512]{1,0:T(8,128)(2,1)} %query_ref.1, bf16[128,512]{1,0:T(8,128)(2,1)} %key_ref.1, bf16[128,4096]{1,0:T(8,128)(2,1)} %v_hbm.1, f32[3,512]{1,0:T(4,128)} %taps_query.1, f32[3,512]{1,0:T(4,128)} %taps_key.1, f32[3,4096]{1,0:T(4,128)} %taps_v.1), custom_call_target="tpu_custom_call" | custom-call | tf_op jit(solution)/shard_map/pallas_call | solution.py:417
  74.7 2.3 %copy.8 = bf16[128,4096]{1,0:T(8,128)(2,1)} copy(bf16[128,4096]{1,0:T(8,128)(2,1)} %shard_map.64) | data formatting | bytes 2097152

commit v3 on v2

--- a/solution.py
+++ b/solution.py
@@ -55,7 +55,7 @@
     taps_query,
     taps_key,
     taps_v,
-    out_hbm,
+    out_ref,
     qk_out,
     qk_in,
     v_in,
@@ -327,7 +327,7 @@
     def send_out(h, peer, owner):
         return remote(
             result.at[h, peer],
-            out_hbm.at[:, columns(owner, h)],
+            out_ref.at[:, columns(owner, h)],
             out_send.at[h, peer],
             out_recv.at[h, owner],
             (s, peer),
@@ -335,7 +335,7 @@
 
     def own_out(h):
         return pltpu.make_async_copy(
-            result.at[h, y], out_hbm.at[:, columns(y, h)], own_out_sem.at[h]
+            result.at[h, y], out_ref.at[:, columns(y, h)], own_out_sem.at[h]
         )
 
     def finish(h):
@@ -418,7 +418,7 @@
         functools.partial(kernel, shards, groups, heads),
         out_shape=jax.ShapeDtypeStruct(value_proj.shape, bf16),
         in_specs=[whole, whole, pl.BlockSpec(memory_space=pl.ANY), whole, whole, whole],
-        out_specs=pl.BlockSpec(memory_space=pl.ANY),
+        out_specs=whole,
         scratch_shapes=[
             scratch((groups, tokens, 2 * heads * KD), bf16),
             scratch((groups + 1, tokens, 2 * heads * KD), bf16),

time: 77.2 us -> 78.2 us (1.013)
  Pallas kernels: 74.7 us -> 75.7 us
    pallas_call x1, Pallas kernels: 74.7 us -> 75.7 us  [on_device(): pl.pallas_call(functools.partial(kernel, shards, groups, heads), out_shap...]
where the time goes in v3:
time: 78.2 us; the launch traced here: 78 us
  Pallas kernels  75.7 us (97%)
  local copies, waits for them, and re-layouts  2.29 us (3%)
    pallas_call x1, Pallas kernels, on_device(): pl.pallas_call(functools.partial(kernel, shards, groups, heads), out_shap...  75.7 us
    unnamed x1, local copies, waits for them, and re-layouts  2.29 us

profile of v3, /device:TPU:1, one launch (start us, length us, event | category | flops | bytes accessed | tf_op | source)
XLA Modules:
  0.0 78.0 jit_solution(6067952143765120329)
XLA Ops:
  0.0 75.7 %shard_map.64 = bf16[128,4096]{1,0:T(8,128)(2,1)} custom-call(bf16[128,512]{1,0:T(8,128)(2,1)} %query_ref.1, bf16[128,512]{1,0:T(8,128)(2,1)} %key_ref.1, bf16[128,4096]{1,0:T(8,128)(2,1)} %v_hbm.1, f32[3,512]{1,0:T(4,128)} %taps_query.1, f32[3,512]{1,0:T(4,128)} %taps_key.1, f32[3,4096]{1,0:T(4,128)} %taps_v.1), custom_call_target="tpu_custom_call" | custom-call | tf_op jit(solution)/shard_map/pallas_call | solution.py:417
  75.7 2.3 %copy.8 = bf16[128,4096]{1,0:T(8,128)(2,1)} copy(bf16[128,4096]{1,0:T(8,128)(2,1)} %shard_map.64) | data formatting | bytes 2097152

commit v4 on v2

--- a/solution.py
+++ b/solution.py
@@ -11,7 +11,7 @@
 VD = 128
 SPAN = 128
 KERNEL = 3
-HALO = 16
+HALO = 8
 FEAT = 160
 PLANE = 8
 MESH = pl.DeviceIdType.MESH

time: 77.2 us -> 75.6 us (0.979)
  Pallas kernels: 74.7 us -> 73.2 us
    pallas_call x1, Pallas kernels: 74.7 us -> 73.2 us  [on_device(): pl.pallas_call(functools.partial(kernel, shards, groups, heads), out_shap...]
where the time goes in v4:
time: 75.6 us; the launch traced here: 75.5 us
  Pallas kernels  73.2 us (97%)
  local copies, waits for them, and re-layouts  2.29 us (3%)
    pallas_call x1, Pallas kernels, on_device(): pl.pallas_call(functools.partial(kernel, shards, groups, heads), out_shap...  73.2 us
    unnamed x1, local copies, waits for them, and re-layouts  2.29 us

profile of v4, /device:TPU:1, one launch (start us, length us, event | category | flops | bytes accessed | tf_op | source)
XLA Modules:
  0.0 75.5 jit_solution(11620702684021949441)
XLA Ops:
  0.0 73.2 %shard_map.64 = bf16[128,4096]{1,0:T(8,128)(2,1)} custom-call(bf16[128,512]{1,0:T(8,128)(2,1)} %query_ref.1, bf16[128,512]{1,0:T(8,128)(2,1)} %key_ref.1, bf16[128,4096]{1,0:T(8,128)(2,1)} %v_hbm.1, f32[3,512]{1,0:T(4,128)} %taps_query.1, f32[3,512]{1,0:T(4,128)} %taps_key.1, f32[3,4096]{1,0:T(4,128)} %taps_v.1), custom_call_target="tpu_custom_call" | custom-call | tf_op jit(solution)/shard_map/pallas_call | solution.py:417
  73.2 2.3 %copy.8 = bf16[128,4096]{1,0:T(8,128)(2,1)} copy(bf16[128,4096]{1,0:T(8,128)(2,1)} %shard_map.64) | data formatting | bytes 2097152
